TPU v7x, 32 devices: a whole 2x2x4 slice. The times are simulated.
32 devices in a mesh: col: 4 (over y, x), row: 8 (over z, core).
Axes of the slice: x: 2, y: 2, z: 4, core: 2. Of those that a mesh axis runs over, the one named last changes fastest.
Arguments:
- snapshots: bfloat16 [8192, 4096], P('row', 'col'), may hold values from -54 to 54
- rotations: bfloat16 [2, 4096, 1024], P(None, 'col'), may hold values from -1 to 2
Outputs:
- gram_first: float32 [4096, 1024], P(('col', 'row'))
- gram_second: float32 [4096, 1024], P(('col', 'row'))
- shrunk: bfloat16 [8192, 4096], P('row', 'col')
All inputs are finite; a program needn't handle non-finite values.
Results may differ from a plain program's by a relative error of at most 0.012.
Values may be sent and summed in bfloat16 or wider, within the bound.
A program may use at most 64 MiB of HBM per device.

v0:
```python
import jax
import jax.numpy as jnp
from jax import lax
from jax.sharding import PartitionSpec as P


def passed_along(value, axis, steps):
    count = lax.axis_size(axis)
    pairs = [(source, (source + steps) % count) for source in range(count)]
    return lax.ppermute(value, axis, pairs)


def gram_term(pair_cols):
    return lax.dot_general(
        pair_cols, pair_cols, (((0,), (0,)), ((), ())), preferred_element_type=jnp.float32
    )


def per_device(snapshots, rotations):
    total_rows = snapshots.shape[0] * lax.axis_size("row")
    block_width = snapshots.shape[1] // 2
    gram_first = (
        lax.psum_scatter(
            gram_term(snapshots).astype(jnp.bfloat16), "row", scatter_dimension=0, tiled=True
        ).astype(jnp.float32)
        / total_rows
    )
    rot_first = rotations[0]
    rot_second = rotations[1]
    turned = jnp.dot(snapshots, rot_first, preferred_element_type=jnp.float32).astype(jnp.bfloat16)
    left_new = turned[:, :block_width]
    right_new = turned[:, block_width:]
    arrived = passed_along(left_new, "col", 1)
    second_pair = jnp.concatenate([arrived, right_new], axis=1)
    moved = jnp.dot(second_pair, rot_second, preferred_element_type=jnp.float32)
    square_sums = jnp.sum(moved * moved, axis=0)
    gram_second = (
        lax.psum_scatter(
            gram_term(second_pair).astype(jnp.bfloat16), "row", scatter_dimension=0, tiled=True
        ).astype(jnp.float32)
        / total_rows
    )
    energy = lax.psum(square_sums, "row")
    singular = jnp.sqrt(energy / total_rows + 1e-06)
    factor = jnp.maximum(singular - 1.8, 0.0) / singular
    shrunk = (moved * factor).astype(jnp.bfloat16)
    return (gram_first, gram_second, shrunk)


def solution(mesh):
    return jax.shard_map(
        per_device,
        mesh=mesh,
        in_specs=(P("row", "col"), P(None, "col", None)),
        out_specs=(P(("col", "row"), None), P(("col", "row"), None), P("row", "col")),
        check_vma=False,
    )
```

profile of v0, /device:TPU:0, one launch (start us, length us, event | category | flops | bytes accessed | tf_op | source)
XLA Modules:
  0.0 96.3 jit_solution(9499575407895095668)
XLA Ops:
  7.2 0.0 copy-start
  7.2 0.0 reduce-scatter.3.cloned.1.call-start
  7.2 1.5 %copy-done = bf16[1024,1024]{1,0:T(8,128)(2,1)S(1)} copy-done((bf16[1024,1024]{1,0:T(8,128)(2,1)S(1)}, bf16[1024,1024]{1,0:T(8,128)(2,1)}, u32[]{:S(2)}) %copy-start) | copy-done | bytes 2097176
  8.8 3.7 %convolution_convert_fusion.1 = bf16[1024,1024]{1,0:T(8,128)(2,1)} fusion(bf16[1024,1024]{1,0:T(8,128)(2,1)S(1)} %copy-done), kind=kOutput, calls=%fused_computation.11 | convolution fusion | flops 2148532224 | bytes 4194304 | tf_op jit(solution)/shard_map/dot_general | solution.py:14
  12.5 0.0 reduce-scatter.3.cloned.1.call-update
  12.5 0.0 reduce-scatter.5.cloned.1.call-start
  12.5 4.0 %fusion.6 = bf16[1024,1024]{0,1:T(8,128)(2,1)S(1)} fusion(bf16[1024,1024]{1,0:T(8,128)(2,1)S(1)} %copy-done, bf16[2,1024,1024]{2,1,0:T(8,128)(2,1)} %param.3), kind=kOutput, calls=%fused_computation.9 | convolution fusion | flops 2148532224 | bytes 6291456 | tf_op jit(solution)/shard_map/dot_general | solution.py:30
  16.5 0.2 fusion.11
  16.7 3.0 %collective-permute-start = (bf16[1024,512]{0,1:T(8,128)(2,1)S(1)}, bf16[1024,512]{0,1:T(8,128)(2,1)S(1)}, u32[]{:S(2)}, u32[]{:S(2)}) collective-permute-start(bf16[1024,512]{0,1:T(8,128)(2,1)S(1)} %get-tuple-element.3), channel_id=1, source_target_pairs={{0,8},{8,16},{16,24},{24,0},{1,9},{9,17},{17,25},{25,1},{2,10},{10... | collective-permute-start | bytes 3145736 | tf_op jit(solution)/shard_map/ppermute | solution.py:10
  19.7 24.1 %collective-permute-done = bf16[1024,512]{0,1:T(8,128)(2,1)S(1)} collective-permute-done((bf16[1024,512]{0,1:T(8,128)(2,1)S(1)}, bf16[1024,512]{0,1:T(8,128)(2,1)S(1)}, u32[]{:S(2)}, u32[]{:S(2)}) %collective-permute-start) | collective-permute-done | bytes 1048608 | tf_op jit(solution)/shard_map/ppermute | solution.py:10
  43.8 0.0 copy-start.1
  43.8 1.0 %copy-done.1 = bf16[1024,512]{0,1:T(8,128)(2,1)} copy-done((bf16[1024,512]{0,1:T(8,128)(2,1)}, bf16[1024,512]{0,1:T(8,128)(2,1)S(1)}, u32[]{:S(2)}) %copy-start.1) | copy-done | bytes 1048600
  44.8 3.7 %convolution_convert_fusion = bf16[1024,1024]{1,0:T(8,128)(2,1)} fusion(bf16[1024,512]{0,1:T(8,128)(2,1)S(1)} %get-tuple-element.4, bf16[1024,512]{0,1:T(8,128)(2,1)S(1)} %collective-permute-done), kind=kOutput, calls=%fused_computation.10 | convolution fusion | flops 2152726528 | bytes 4194304 | tf_op jit(solution)/shard_map/dot_general | solution.py:14
  48.5 0.0 reduce-scatter.5.cloned.1.call-update
  48.5 6.3 %multiply_reduce_fusion = (f32[1024]{0:T(1024)S(1)}, f32[1024,1024]{1,0:T(8,128)}) fusion(bf16[2,1024,1024]{2,1,0:T(8,128)(2,1)} %param.3, bf16[1024,512]{0,1:T(8,128)(2,1)S(1)} %get-tuple-element.4, bf16[1024,512]{0,1:T(8,128)(2,1)} %copy-done.1), kind=kOutput, calls=%fused_computation.1 | convolution fusion | flops 2153774080 | bytes 8392704 | tf_op jit(solution)/shard_map/dot_general | solution.py:35
  54.8 16.2 %psum.7 = f32[1024]{0:T(1024)S(1)} all-reduce(f32[1024]{0:T(1024)S(1)} %get-tuple-element.5), channel_id=1, replica_groups=mesh['col'=4,'row'=8] {'row'}, use_global_device_ids=true, to_apply=%region_3.0 | all-reduce | flops 1024 | bytes 8192 | tf_op jit(solution)/shard_map/psum | solution.py:43
  71.0 4.2 %multiply_convert_fusion = bf16[1024,1024]{1,0:T(8,128)(2,1)} fusion(f32[1024,1024]{1,0:T(8,128)} %get-tuple-element.6, f32[1024]{0:T(1024)S(1)} %maximum_divide_fusion), kind=kLoop, calls=%fused_computation | loop fusion | flops 2097152 | bytes 6295552 | tf_op jit(solution)/shard_map/convert_element_type | solution.py:46
  75.1 0.0 reduce-scatter.3.cloned.1.call-done
  75.1 1.8 %convert_multiply_fusion.1 = f32[128,1024]{1,0:T(8,128)} fusion(bf16[128,1024]{1,0:T(8,128)(2,1)} %reduce-scatter.3.cloned.1.call-done), kind=kLoop, calls=%fused_computation.13 | loop fusion | flops 262144 | bytes 786432 | tf_op jit(solution)/shard_map/div | solution.py:23
  76.9 10.8 %reduce-scatter.5.cloned.1.call-done = bf16[128,1024]{1,0:T(8,128)(2,1)} async-done(((bf16[1024,1024]{1,0:T(8,128)(2,1)}), bf16[128,1024]{1,0:T(8,128)(2,1)}) %reduce-scatter.5.cloned.1.call-update) | async-done | bytes 262160 | tf_op jit(solution)/shard_map/reduce_scatter | solution.py:38
  87.7 1.8 %convert_multiply_fusion = f32[128,1024]{1,0:T(8,128)} fusion(bf16[128,1024]{1,0:T(8,128)(2,1)} %reduce-scatter.5.cloned.1.call-done), kind=kLoop, calls=%fused_computation.12 | loop fusion | flops 262144 | bytes 786432 | tf_op jit(solution)/shard_map/div | solution.py:38
  (1 shorter events, 0.0 us)
Async XLA Ops:
  7.2 1.6 %copy-start = (bf16[1024,1024]{1,0:T(8,128)(2,1)S(1)}, bf16[1024,1024]{1,0:T(8,128)(2,1)}, u32[]{:S(2)}) copy-start(bf16[1024,1024]{1,0:T(8,128)(2,1)} %param.2) | copy-start | bytes 6291460
  7.2 67.9 %reduce-scatter.3.cloned.1.call-start = ((), (), s32[]{:S(2)}) async-start(), calls=%async_computation.2 | async-start | bytes 2359296 | tf_op jit(solution)/shard_map/reduce_scatter | solution.py:23
  12.5 75.2 %reduce-scatter.5.cloned.1.call-start = ((), (), s32[]{:S(2)}) async-start(), calls=%async_computation.3 | async-start | bytes 2359296 | tf_op jit(solution)/shard_map/reduce_scatter | solution.py:38
  16.7 27.1 %collective-permute-start = (bf16[1024,512]{0,1:T(8,128)(2,1)S(1)}, bf16[1024,512]{0,1:T(8,128)(2,1)S(1)}, u32[]{:S(2)}, u32[]{:S(2)}) collective-permute-start(bf16[1024,512]{0,1:T(8,128)(2,1)S(1)} %get-tuple-element.3), channel_id=1, source_target_pairs={{0,8},{8,16},{16,24},{24,0},{1,9},{9,17},{17,25},{25,1},{2,10},{10... | collective-permute-start | bytes 3145736 | tf_op jit(solution)/shard_map/ppermute | solution.py:10
  43.8 1.0 %copy-start.1 = (bf16[1024,512]{0,1:T(8,128)(2,1)}, bf16[1024,512]{0,1:T(8,128)(2,1)S(1)}, u32[]{:S(2)}) copy-start(bf16[1024,512]{0,1:T(8,128)(2,1)S(1)} %collective-permute-done) | copy-start | bytes 3145732
Sparse Core Ops, SparseCore 0:
  12.6 38.3 reduce-scatter.2
  53.3 34.3 reduce-scatter.4
where the time goes:
time: 96.6 us; the launch traced here: 96.3 us
  waiting for transfers between devices  34.9 us (36%)
  matrix products  17.7 us (18%)
  blocking collectives  16.2 us (17%)
  between operations  14.1 us (15%)
  other arithmetic  7.76 us (8%)
  starting transfers between devices  3.07 us (3%)
  local copies, waits for them, and re-layouts  2.69 us (3%)
    ppermute x1, waiting for transfers between devices, passed_along(): return lax.ppermute(value, axis, pairs)  24.1 us
    psum x1, blocking collectives, per_device(): energy = lax.psum(square_sums, 'row')  16.2 us
    reduce_scatter x1, waiting for transfers between devices, per_device(): lax.psum_scatter(gram_term(second_pair).astype(jnp.bfloat16), 'row', scat...  10.8 us
    dot_general x2, matrix products, gram_term(): lax.dot_general(pair_cols, pair_cols, (((0,), (0,)), ((), ())), preferred...  7.42 us
    dot_general x1, matrix products, per_device(): moved = jnp.dot(second_pair, rot_second, preferred_element_type=jnp.float32)  6.26 us
    convert_element_type x1, other arithmetic, per_device(): shrunk = (moved * factor).astype(jnp.bfloat16)  4.15 us
    dot_general x1, matrix products, per_device(): jnp.dot(snapshots, rot_first, preferred_element_type=jnp.float32)  3.98 us
    ppermute x1, starting transfers between devices, passed_along(): return lax.ppermute(value, axis, pairs)  2.99 us
  transfers between devices with their start and end apart: 3, of which 2 were waited for; matrix products, arithmetic and copies ran while one was open for 21% of the time, Pallas kernels for 0%

commit v1 on v0

v1 whole, which is shorter than its diff:
```python
import functools

import jax
import jax.numpy as jnp
from jax import lax
from jax.experimental import pallas as pl
from jax.experimental.pallas import tpu as pltpu
from jax.sharding import PartitionSpec as P

TILE = 256
LANE = 128


def kernel(
    n, n_col, x_hbm, rot_hbm, g1_hbm, g2_hbm, out_hbm,
    x, rot, left, pair, moved, part, peer, sums, landed, turn_out, turn_in,
    gram_out, energy, energy_in, shrunk,
    load_sem, left_send, left_recv, core_send, core_recv, z_send, z_recv,
    turn_send, turn_recv, e_send, e_recv, store_sem, shrunk_sem,
):
    rows, width = x.shape
    half = width // 2
    block = width // n
    groups = n // 2
    symmetric = block == LANE
    total_rows = rows * n
    tiles = width // TILE
    row_tiles = rows // TILE
    per_tile = TILE // (2 * block)
    turns = n // 2 - 1 if symmetric else 0

    me_col = lax.axis_index("col")
    me = lax.axis_index("row")
    core = lax.rem(me, 2)
    group = lax.div(me, 2)
    partner = me + 1 - 2 * core

    def peer_at(step):
        return lax.rem(me + step, n)

    load_x = pltpu.make_async_copy(x_hbm, x, load_sem.at[0])
    load_r0 = [
        pltpu.make_async_copy(
            rot_hbm.at[0, :, pl.ds(h * half, half)], rot.at[0, :, pl.ds(h * half, half)],
            load_sem.at[1 + h],
        )
        for h in range(2)
    ]
    load_r1 = pltpu.make_async_copy(rot_hbm.at[1], rot.at[1], load_sem.at[3])
    load_x.start()
    load_r0[0].start()
    load_r0[1].start()
    load_r1.start()

    following = lax.rem(me_col + 1, n_col)
    preceding = lax.rem(me_col + n_col - 1, n_col)
    barrier = pltpu.get_barrier_semaphore()
    for other in (following, preceding):
        pl.semaphore_signal(
            barrier, inc=1, device_id={"col": other, "row": me},
            device_id_type=pl.DeviceIdType.MESH,
        )
    for step in range(1, n):
        pl.semaphore_signal(
            barrier, inc=1, device_id={"col": me_col, "row": peer_at(step)},
            device_id_type=pl.DeviceIdType.MESH,
        )

    def remote(src, dst, send_sem, recv_sem, col, row):
        return pltpu.make_async_remote_copy(
            src_ref=src, dst_ref=dst, send_sem=send_sem, recv_sem=recv_sem,
            device_id={"col": col, "row": row}, device_id_type=pl.DeviceIdType.MESH,
        )

    def turn(into, first, column):
        def body(t, _):
            span = pl.ds(pl.multiple_of(t * TILE, TILE), TILE)
            into[span, pl.ds(column - first, TILE)] = jnp.dot(
                x[span, :], rot[0, :, pl.ds(column, TILE)], preferred_element_type=jnp.float32
            ).astype(jnp.bfloat16)
            return 0
        lax.fori_loop(0, row_tiles, body, 0)

    pieces = half // TILE
    left_copy = [
        remote(
            left.at[:, pl.ds(h * TILE, TILE)], pair.at[:, pl.ds(h * TILE, TILE)],
            left_send.at[h], left_recv.at[h], following, me,
        )
        for h in range(pieces)
    ]
    load_x.wait()
    load_r0[0].wait()
    for h in range(pieces):
        turn(left, 0, h * TILE)
        if h == 0:
            pl.semaphore_wait(barrier, n + 1)
        left_copy[h].start()

    def core_copy(s, q):
        span = pl.ds(q * per_tile, per_tile)
        return remote(
            part.at[s, 1 - core, span], peer.at[s, span],
            core_send.at[s, q], core_recv.at[s, q], me_col, partner,
        )

    def z_copy(s, k, g):
        return remote(
            sums.at[s, g], landed.at[s, k - 1], z_send.at[s, k - 1], z_recv.at[s, k - 1],
            me_col, 2 * g + core,
        )

    def gram_terms(s, source):
        def body(step, _):
            q = lax.rem(group + 1 + step, tiles) if symmetric else step
            columns = pl.ds(pl.multiple_of(q * TILE, TILE), TILE)
            flipped = source[:, columns].T
            for m in range(3 if symmetric else tiles):
                c = lax.rem(q + m, tiles) if symmetric else m
                term = jnp.dot(
                    flipped, source[:, pl.ds(pl.multiple_of(c * TILE, TILE), TILE)],
                    preferred_element_type=jnp.float32,
                ).astype(jnp.bfloat16)
                if symmetric:
                    lo = m * TILE
                    wide = TILE if m < 2 else LANE
                    part[s, 0, q, :, lo:lo + wide] = term[:LANE, :wide]
                    if m == 0:
                        part[s, 1, q, :, 0:LANE] = term[LANE:, LANE:]
                    else:
                        part[s, 1, q, :, lo - LANE:lo - LANE + TILE] = term[LANE:, :]
                else:
                    for e in range(2 * per_tile):
                        part[s, e % 2, q * per_tile + e // 2, :, m * TILE:(m + 1) * TILE] = term[
                            e * block:(e + 1) * block, :
                        ]
            core_copy(s, q).start()
            return 0
        lax.fori_loop(0, tiles, body, 0)

    def gram_pass(s):
        if not symmetric:
            for q in range(tiles):
                core_copy(s, q).wait_recv()
        def body(k, _):
            g = lax.rem(group + k, groups)
            if symmetric:
                core_copy(s, g).wait_recv()
            sums[s, g] = (
                part[s, core, g].astype(jnp.float32) + peer[s, g].astype(jnp.float32)
            ).astype(jnp.bfloat16)
            z_copy(s, k, g).start()
            return 0
        lax.fori_loop(1, groups, body, 0)

    def turn_copy(s, d):
        return remote(
            turn_out.at[s, d - 1], turn_in.at[s, d - 1],
            turn_send.at[s, d - 1], turn_recv.at[s, d - 1], me_col, peer_at(d),
        )

    def gram_sum(s):
        if symmetric:
            core_copy(s, group).wait_recv()
        for k in range(1, groups):
            z_copy(s, k, lax.rem(group + k, groups)).wait_recv()
        for d in range(part.shape[-1] // LANE):
            span = pl.ds(d * LANE, LANE)
            total = part[s, core, group, :, span].astype(jnp.float32) + peer[
                s, group, :, span
            ].astype(jnp.float32)
            for k in range(1, groups):
                total = total + landed[s, k - 1, :, span].astype(jnp.float32)
            total = total / total_rows
            if symmetric:
                if 1 <= d <= turns:
                    turn_out[s, d - 1] = total.T.astype(jnp.bfloat16)
                    turn_copy(s, d).start()
                at = pl.ds(pl.multiple_of(peer_at(d) * LANE, LANE), LANE)
                gram_out[s, :, at] = total
            else:
                gram_out[s, :, span] = total

    def gram_end(s, target):
        for d in range(1, turns + 1):
            turn_copy(s, d).wait_recv()
            at = pl.ds(pl.multiple_of(peer_at(n - d) * LANE, LANE), LANE)
            gram_out[s, :, at] = turn_in[s, d - 1].astype(jnp.float32)
        copy = pltpu.make_async_copy(gram_out.at[s], target, store_sem.at[s])
        copy.start()
        return copy

    gram_terms(0, x)
    load_r0[1].wait()
    for h in range(pieces):
        turn(pair, 0, half + h * TILE)
    gram_pass(0)

    load_r1.wait()

    def add_moved(first, depth, fresh):
        def body(t, acc):
            span = pl.ds(pl.multiple_of(t * TILE, TILE), TILE)
            value = jnp.dot(
                pair[span, pl.ds(first, depth)], rot[1, pl.ds(first, depth), :],
                preferred_element_type=jnp.float32,
            )
            if not fresh:
                value = value + moved[span, :]
            moved[span, :] = value
            return acc + jnp.sum(value * value, axis=0, keepdims=True)
        return lax.fori_loop(0, row_tiles, body, jnp.zeros((1, width), jnp.float32))

    add_moved(half, half, True)
    gram_sum(0)
    first_store = gram_end(0, g1_hbm)

    for h in range(pieces - 1):
        left_copy[h].wait_recv()
        add_moved(h * TILE, TILE, False)
    left_copy[pieces - 1].wait_recv()
    gram_terms(1, pair)
    energy[...] = add_moved(half - TILE, TILE, False)

    def e_copy(step):
        return remote(
            energy, energy_in.at[step - 1], e_send.at[step - 1], e_recv.at[step - 1],
            me_col, peer_at(step),
        )

    for step in range(1, n):
        e_copy(step).start()
    gram_pass(1)
    total = energy[...]
    for step in range(1, n):
        e_copy(step).wait_recv()
        total = total + energy_in[step - 1]
    singular = jnp.sqrt(total / total_rows + 1e-06)
    factor = jnp.maximum(singular - 1.8, 0.0) / singular

    def out_copy(t):
        span = pl.ds(pl.multiple_of(t * TILE, TILE), TILE)
        return pltpu.make_async_copy(shrunk.at[span, :], out_hbm.at[span, :], shrunk_sem.at[t])

    def shrink(t, _):
        span = pl.ds(pl.multiple_of(t * TILE, TILE), TILE)
        shrunk[span, :] = (moved[span, :] * factor).astype(jnp.bfloat16)
        out_copy(t).start()
        return 0

    lax.fori_loop(0, row_tiles, shrink, 0)
    gram_sum(1)
    second_store = gram_end(1, g2_hbm)

    for h in range(pieces):
        left_copy[h].wait_send()
    for s in range(2):
        for q in range(tiles):
            core_copy(s, q).wait_send()
        for k in range(1, groups):
            z_copy(s, k, lax.rem(group + k, groups)).wait_send()
        for d in range(1, turns + 1):
            turn_copy(s, d).wait_send()
    for step in range(1, n):
        e_copy(step).wait_send()
    for t in range(row_tiles):
        out_copy(t).wait()
    first_store.wait()
    second_store.wait()


def per_device(n, n_col, snapshots, rotations):
    rows, width = snapshots.shape
    half = width // 2
    block = width // n
    groups = n // 2
    tiles = width // TILE
    symmetric = block == LANE
    reach = (groups + 1) * LANE if symmetric else width
    turns = groups - 1 if symmetric else 1
    bf16, f32, dma = jnp.bfloat16, jnp.float32, pltpu.SemaphoreType.DMA
    anywhere = pl.BlockSpec(memory_space=pl.ANY)
    return pl.pallas_call(
        functools.partial(kernel, n, n_col),
        out_shape=(
            jax.ShapeDtypeStruct((block, width), f32),
            jax.ShapeDtypeStruct((block, width), f32),
            jax.ShapeDtypeStruct((rows, width), bf16),
        ),
        in_specs=[anywhere] * 2,
        out_specs=(anywhere,) * 3,
        scratch_shapes=[
            pltpu.VMEM((rows, width), bf16),
            pltpu.VMEM((2, width, width), bf16),
            pltpu.VMEM((rows, half), bf16),
            pltpu.VMEM((rows, width), bf16),
            pltpu.VMEM((rows, width), f32),
            pltpu.VMEM((2, 2, groups, block, reach), bf16),
            pltpu.VMEM((2, groups, block, reach), bf16),
            pltpu.VMEM((2, groups, block, reach), bf16),
            pltpu.VMEM((2, groups - 1, block, reach), bf16),
            pltpu.VMEM((2, turns, LANE, LANE), bf16),
            pltpu.VMEM((2, turns, LANE, LANE), bf16),
            pltpu.VMEM((2, block, width), f32),
            pltpu.VMEM((1, width), f32),
            pltpu.VMEM((n - 1, 1, width), f32),
            pltpu.VMEM((rows, width), bf16),
            dma((4,)),
            dma((half // TILE,)),
            dma((half // TILE,)),
            dma((2, tiles)),
            dma((2, tiles)),
            dma((2, groups - 1)),
            dma((2, groups - 1)),
            dma((2, turns)),
            dma((2, turns)),
            dma((n - 1,)),
            dma((n - 1,)),
            dma((2,)),
            dma((rows // TILE,)),
        ],
        compiler_params=pltpu.CompilerParams(
            collective_id=0, has_side_effects=True, vmem_limit_bytes=56 * 1024 * 1024
        ),
    )(snapshots, rotations)


def solution(mesh):
    return jax.shard_map(
        functools.partial(per_device, mesh.shape["row"], mesh.shape["col"]),
        mesh=mesh,
        in_specs=(P("row", "col"), P(None, "col", None)),
        out_specs=(P(("col", "row"), None), P(("col", "row"), None), P("row", "col")),
        check_vma=False,
    )
```

time: 96.6 us -> 63.8 us (0.66)
  Pallas kernels: 0 us -> 57.7 us
  waiting for transfers between devices: 34.9 us -> 0 us
  matrix products: 17.7 us -> 0 us
  blocking collectives: 16.2 us -> 0 us
  between operations: 14.1 us -> 0.65 us
  other arithmetic: 7.76 us -> 0 us
  starting transfers between devices: 3.07 us -> 0 us
  local copies, waits for them, and re-layouts: 2.69 us -> 5.24 us
    pallas_call x0 -> x1, Pallas kernels: none -> 57.7 us  [per_device(): pl.pallas_call(functools.partial(kernel, n, n_col), out_shape=(jax.ShapeD...]
    ppermute x1 -> x0, waiting for transfers between devices: 24.1 us -> none  [passed_along(): return lax.ppermute(value, axis, pairs)]
    dot_general x4 -> x0, matrix products: 17.7 us -> none  [the longest x2 7.42 us: gram_term(): lax.dot_general(pair_cols, pair_cols, (((0,), (0,)), ((), ())), preferred...]
    psum x1 -> x0, blocking collectives: 16.2 us -> none  [per_device(): energy = lax.psum(square_sums, 'row')]
    reduce_scatter x2 -> x0, waiting for transfers between devices: 10.8 us -> none  [the longest x1 10.8 us: per_device(): lax.psum_scatter(gram_term(second_pair).astype(jnp.bfloat16), 'row', scat...]
    convert_element_type x1 -> x0, other arithmetic: 4.15 us -> none  [per_device(): shrunk = (moved * factor).astype(jnp.bfloat16)]
    div x3 -> x0, other arithmetic: 3.61 us -> none  [the longest x1 1.8 us: per_device(): lax.psum_scatter(gram_term(snapshots).astype(jnp.bfloat16), 'row', scatte...]
    ppermute x1 -> x0, starting transfers between devices: 2.99 us -> none  [passed_along(): return lax.ppermute(value, axis, pairs)]
  transfers between devices with their start and end apart: 3 -> 0, of which waited for: 2 -> 0; matrix products, arithmetic and copies ran while one was open for 21% -> 0% of each run, Pallas kernels for 0% -> 0%
where the time goes in v1:
time: 63.8 us; the launch traced here: 63.6 us
  Pallas kernels  57.7 us (90%)
  local copies, waits for them, and re-layouts  5.24 us (8%)
  between operations  0.65 us (1%)
    pallas_call x1, Pallas kernels, per_device(): pl.pallas_call(functools.partial(kernel, n, n_col), out_shape=(jax.ShapeD...  57.7 us
    unnamed x5, local copies, waits for them, and re-layouts  5.24 us

profile of v1, /device:TPU:0, one launch (start us, length us, event | category | flops | bytes accessed | tf_op | source)
XLA Modules:
  0.0 63.6 jit_solution(3224186085645555214)
XLA Ops:
  0.6 57.7 %shard_map.49 = (f32[128,1024]{1,0:T(8,128)}, f32[128,1024]{1,0:T(8,128)}, bf16[1024,1024]{1,0:T(8,128)(2,1)}) custom-call(bf16[1024,1024]{1,0:T(8,128)(2,1)} %x_hbm.1, bf16[2,1024,1024]{2,1,0:T(8,128)(2,1)} %rot_hbm.1), custom_call_target="tpu_custom_call" | custom-call | tf_op jit(solution)/shard_map/pallas_call | solution.py:283
  58.4 0.0 copy-start
  58.4 2.0 %copy.8 = f32[128,1024]{1,0:T(8,128)} copy(f32[128,1024]{1,0:T(8,128)} %get-tuple-element.6) | data formatting | bytes 1048576
  60.4 1.9 %copy.9 = f32[128,1024]{1,0:T(8,128)} copy(f32[128,1024]{1,0:T(8,128)} %get-tuple-element.7) | data formatting | bytes 1048576
  62.3 0.0 copy-done
  62.3 1.3 %copy.10 = bf16[1024,1024]{1,0:T(8,128)(2,1)} copy(bf16[1024,1024]{1,0:T(8,128)(2,1)S(1)} %copy-done) | data formatting | bytes 4194304
Async XLA Ops:
  58.4 3.9 %copy-start = (bf16[1024,1024]{1,0:T(8,128)(2,1)S(1)}, bf16[1024,1024]{1,0:T(8,128)(2,1)}, u32[]{:S(2)}) copy-start(bf16[1024,1024]{1,0:T(8,128)(2,1)} %get-tuple-element.8) | copy-start | bytes 6291460

commit v2 on v1

v2 whole, which is shorter than its diff:
```python
import functools

import jax
import jax.numpy as jnp
from jax import lax
from jax.experimental import pallas as pl
from jax.experimental.pallas import tpu as pltpu
from jax.sharding import PartitionSpec as P

TILE = 256
LANE = 128

UNITS = ((0, 0), (0, 2), (0, 3), (0, 1), (2, 2), (2, 3), (2, 1), (3, 3), (3, 1), (1, 1))
FIRST = (0, 1, 2, 3, 4, 5, 6, 7, 8, 9)
STAGES = ((4, 5, 7), (0, 1, 2), (3, 6, 8, 9))


def kernel(
    n, n_col, x_hbm, rot_hbm, g1_hbm, g2_hbm, out_hbm,
    x, rot, left, pair, moved, part, peer, sums, landed, turn_out, turn_in,
    gram_out, energy, energy_in, shrunk,
    flipped, load_sem, left_send, left_recv, core_send, core_recv, z_send, z_recv,
    turn_send, turn_recv, e_send, e_recv, store_sem, shrunk_sem,
):
    rows, width = x.shape
    half = width // 2
    block = width // n
    groups = n // 2
    symmetric = n == 8 and block == LANE
    total_rows = rows * n
    tiles = width // TILE
    row_tiles = rows // TILE
    per_tile = TILE // (2 * block)

    me_col = lax.axis_index("col")
    me = lax.axis_index("row")
    core = lax.rem(me, 2)
    group = lax.div(me, 2)
    partner = me + 1 - 2 * core

    def peer_at(step):
        return lax.rem(me + step, n)

    load_x = pltpu.make_async_copy(x_hbm, x, load_sem.at[0])
    load_r0 = [
        pltpu.make_async_copy(
            rot_hbm.at[0, :, pl.ds(h * half, half)], rot.at[0, :, pl.ds(h * half, half)],
            load_sem.at[1 + h],
        )
        for h in range(2)
    ]
    load_r1 = pltpu.make_async_copy(rot_hbm.at[1], rot.at[1], load_sem.at[3])
    load_x.start()
    load_r0[0].start()
    load_r0[1].start()
    load_r1.start()

    following = lax.rem(me_col + 1, n_col)
    preceding = lax.rem(me_col + n_col - 1, n_col)
    barrier = pltpu.get_barrier_semaphore()
    for other in (following, preceding):
        pl.semaphore_signal(
            barrier, inc=1, device_id={"col": other, "row": me},
            device_id_type=pl.DeviceIdType.MESH,
        )
    for step in range(1, n):
        pl.semaphore_signal(
            barrier, inc=1, device_id={"col": me_col, "row": peer_at(step)},
            device_id_type=pl.DeviceIdType.MESH,
        )

    def remote(src, dst, send_sem, recv_sem, col, row):
        return pltpu.make_async_remote_copy(
            src_ref=src, dst_ref=dst, send_sem=send_sem, recv_sem=recv_sem,
            device_id={"col": col, "row": row}, device_id_type=pl.DeviceIdType.MESH,
        )

    def turn(into, first, column):
        def body(t, _):
            span = pl.ds(pl.multiple_of(t * TILE, TILE), TILE)
            into[span, pl.ds(column - first, TILE)] = jnp.dot(
                x[span, :], rot[0, :, pl.ds(column, TILE)], preferred_element_type=jnp.float32
            ).astype(jnp.bfloat16)
            return 0
        lax.fori_loop(0, row_tiles, body, 0)

    pieces = half // TILE
    left_copy = [
        remote(
            left.at[:, pl.ds(h * TILE, TILE)], pair.at[:, pl.ds(h * TILE, TILE)],
            left_send.at[h], left_recv.at[h], following, me,
        )
        for h in range(pieces)
    ]
    load_x.wait()
    load_r0[0].wait()
    for h in range(pieces):
        turn(left, 0, h * TILE)
        if h == 0:
            pl.semaphore_wait(barrier, n + 1)
        left_copy[h].start()

    def owned(u):
        g = UNITS[u][0]
        return [v for v in range(len(UNITS)) if UNITS[v][0] == g].index(u)

    def core_copy(s, u):
        return remote(
            part.at[s, 1 - core, u], peer.at[s, u],
            core_send.at[s, u], core_recv.at[s, u], me_col, partner,
        )

    def z_copy(s, u):
        g = UNITS[u][0] if symmetric else lax.rem(group + u, groups)
        k = lax.rem(g - group + 2 * groups - 1, groups)
        if symmetric:
            v = owned(u)
            return remote(
                sums.at[s, u], landed.at[s, v, k], z_send.at[s, u], z_recv.at[s, v, k],
                me_col, 2 * g + core,
            )
        return remote(
            sums.at[s, g], landed.at[s, 0, k], z_send.at[s, k], z_recv.at[s, 0, k],
            me_col, 2 * g + core,
        )

    def added(s, u):
        return part[s, core, u].astype(jnp.float32) + peer[s, u].astype(jnp.float32)

    def turn_copy(s, u, e):
        g, c = UNITS[u]
        return remote(
            turn_out.at[s, owned(u), e], turn_in.at[s, g, core],
            turn_send.at[s, owned(u), e], turn_recv.at[s, g, core], me_col, 2 * c + e,
        )

    def flip(source, g):
        flipped[g] = source[:, g * TILE:(g + 1) * TILE].T

    def pair_terms(s, source, units):
        for u in units:
            g, c = UNITS[u]
            term = jnp.dot(
                flipped[g], source[:, c * TILE:(c + 1) * TILE],
                preferred_element_type=jnp.float32,
            ).astype(jnp.bfloat16)
            part[s, 0, u] = term[:LANE]
            part[s, 1, u] = term[LANE:]
            core_copy(s, u).start()

    def pair_pass(s, units):
        for u in units:
            core_copy(s, u).wait_recv()

            @pl.when(group != UNITS[u][0])
            def _():
                sums[s, u] = added(s, u).astype(jnp.bfloat16)
                z_copy(s, u).start()

    def pair_sum(s, units):
        for u in units:
            g, c = UNITS[u]

            @pl.when(group == g)
            def _():
                v = owned(u)
                total = added(s, u)
                for k in range(groups - 1):
                    remote(
                        sums.at[s, u], landed.at[s, v, k], z_send.at[s, u], z_recv.at[s, v, k],
                        me_col, partner,
                    ).wait_recv()
                    total = total + landed[s, v, k].astype(jnp.float32)
                total = total / total_rows
                if c != g:
                    for e in range(2):
                        turn_out[s, v, e] = total[:, e * LANE:(e + 1) * LANE].T.astype(jnp.bfloat16)
                        turn_copy(s, u, e).start()
                gram_out[s, :, c * TILE:(c + 1) * TILE] = total

    def pair_turned(s, units):
        for u in units:
            g, c = UNITS[u]
            if c != g:

                @pl.when(group == c)
                def _():
                    for e in range(2):
                        remote(
                            turn_out.at[s, 0, 0], turn_in.at[s, g, e], turn_send.at[s, 0, 0],
                            turn_recv.at[s, g, e], me_col, partner,
                        ).wait_recv()
                        gram_out[s, :, (2 * g + e) * LANE:(2 * g + e + 1) * LANE] = turn_in[
                            s, g, e
                        ].astype(jnp.float32)

    def pair_drain(s, units):
        for u in units:
            g, c = UNITS[u]
            core_copy(s, u).wait_send()

            @pl.when(group != g)
            def _():
                z_copy(s, u).wait_send()

            if c != g:

                @pl.when(group == g)
                def _():
                    for e in range(2):
                        turn_copy(s, u, e).wait_send()

    def rows_copy(s, q):
        span = pl.ds(q * per_tile, per_tile)
        return remote(
            part.at[s, 1 - core, span], peer.at[s, span],
            core_send.at[s, q], core_recv.at[s, q], me_col, partner,
        )

    def rows_terms(s, source):
        def body(q, _):
            turned_tile = source[:, pl.ds(pl.multiple_of(q * TILE, TILE), TILE)].T
            for m in range(tiles):
                term = jnp.dot(
                    turned_tile, source[:, m * TILE:(m + 1) * TILE],
                    preferred_element_type=jnp.float32,
                ).astype(jnp.bfloat16)
                for e in range(2 * per_tile):
                    part[s, e % 2, q * per_tile + e // 2, :, m * TILE:(m + 1) * TILE] = term[
                        e * block:(e + 1) * block, :
                    ]
            rows_copy(s, q).start()
            return 0
        lax.fori_loop(0, tiles, body, 0)

    def rows_pass(s):
        for q in range(tiles):
            rows_copy(s, q).wait_recv()

        def body(k, _):
            g = lax.rem(group + k, groups)
            sums[s, g] = added(s, g).astype(jnp.bfloat16)
            z_copy(s, k).start()
            return 0
        lax.fori_loop(1, groups, body, 0)

    def rows_sum(s):
        total = added(s, group)
        for k in range(1, groups):
            z_copy(s, k).wait_recv()
            total = total + landed[s, 0, k - 1].astype(jnp.float32)
        gram_out[s] = total / total_rows

    def gram_store(s, target):
        return pltpu.make_async_copy(gram_out.at[s], target, store_sem.at[s])

    if symmetric:
        for g in range(tiles):
            flip(x, g)
            pair_terms(0, x, [u for u in FIRST if UNITS[u][0] == g])
    else:
        rows_terms(0, x)
    load_r0[1].wait()
    for h in range(pieces):
        turn(pair, 0, half + h * TILE)
    if symmetric:
        pair_pass(0, FIRST)
        flip(pair, 2)
        flip(pair, 3)
        pair_terms(1, pair, STAGES[0])
    else:
        rows_pass(0)

    load_r1.wait()

    def add_moved(first, depth, fresh):
        def body(t, acc):
            span = pl.ds(pl.multiple_of(t * TILE, TILE), TILE)
            value = jnp.dot(
                pair[span, pl.ds(first, depth)], rot[1, pl.ds(first, depth), :],
                preferred_element_type=jnp.float32,
            )
            if not fresh:
                value = value + moved[span, :]
            moved[span, :] = value
            return acc + jnp.sum(value * value, axis=0, keepdims=True)
        return lax.fori_loop(0, row_tiles, body, jnp.zeros((1, width), jnp.float32))

    add_moved(half, half, True)
    if symmetric:
        pair_pass(1, STAGES[0])
    left_copy[0].wait_recv()
    if symmetric:
        flip(pair, 0)
        pair_terms(1, pair, STAGES[1])
    for h in range(pieces - 1):
        if h > 0:
            left_copy[h].wait_recv()
        add_moved(h * TILE, TILE, False)
    if symmetric:
        pair_pass(1, STAGES[1])
        pair_sum(0, FIRST)
        pair_turned(0, FIRST)
    else:
        rows_sum(0)
    gram_store(0, g1_hbm).start()
    if symmetric:
        pair_sum(1, STAGES[0])
    left_copy[pieces - 1].wait_recv()
    if symmetric:
        flip(pair, 1)
        pair_terms(1, pair, STAGES[2])
    else:
        rows_terms(1, pair)
    energy[...] = add_moved(half - TILE, TILE, False)

    def e_copy(step):
        return remote(
            energy, energy_in.at[step - 1], e_send.at[step - 1], e_recv.at[step - 1],
            me_col, peer_at(step),
        )

    for step in range(1, n):
        e_copy(step).start()
    if symmetric:
        pair_pass(1, STAGES[2])
        pair_sum(1, STAGES[1])
        pair_turned(1, STAGES[0] + STAGES[1])
    else:
        rows_pass(1)
    total = energy[...]
    for step in range(1, n):
        e_copy(step).wait_recv()
        total = total + energy_in[step - 1]
    singular = jnp.sqrt(total / total_rows + 1e-06)
    factor = jnp.maximum(singular - 1.8, 0.0) / singular

    def out_copy(t):
        span = pl.ds(pl.multiple_of(t * TILE, TILE), TILE)
        return pltpu.make_async_copy(shrunk.at[span, :], out_hbm.at[span, :], shrunk_sem.at[t])

    def shrink(t, _):
        span = pl.ds(pl.multiple_of(t * TILE, TILE), TILE)
        shrunk[span, :] = (moved[span, :] * factor).astype(jnp.bfloat16)
        out_copy(t).start()
        return 0

    lax.fori_loop(0, row_tiles, shrink, 0)
    if symmetric:
        pair_sum(1, STAGES[2])
        pair_turned(1, STAGES[2])
    else:
        rows_sum(1)
    gram_store(1, g2_hbm).start()

    for h in range(pieces):
        left_copy[h].wait_send()
    for s in range(2):
        if symmetric:
            pair_drain(s, FIRST)
        else:
            for q in range(tiles):
                rows_copy(s, q).wait_send()
            for k in range(1, groups):
                z_copy(s, k).wait_send()
    for step in range(1, n):
        e_copy(step).wait_send()
    for t in range(row_tiles):
        out_copy(t).wait()
    gram_store(0, g1_hbm).wait()
    gram_store(1, g2_hbm).wait()


def finish(*refs):
    sources, targets, sem = refs[:3], refs[3:6], refs[6]
    copies = []
    for source, target in zip(sources, targets):
        pieces = 4 if source.shape[0] > 512 else 1
        size = source.shape[0] // pieces
        for p in range(pieces):
            span = pl.ds(p * size, size)
            copies.append(
                pltpu.make_async_copy(source.at[span], target.at[span], sem.at[len(copies)])
            )
    for copy in copies:
        copy.start()
    for copy in copies:
        copy.wait()


def per_device(n, n_col, snapshots, rotations):
    rows, width = snapshots.shape
    half = width // 2
    block = width // n
    groups = n // 2
    tiles = width // TILE
    symmetric = n == 8 and block == LANE
    units = len(UNITS) if symmetric else groups
    reach = TILE if symmetric else width
    owned = 4 if symmetric else 1
    sends = units if symmetric else max(groups - 1, tiles)
    bf16, f32, dma = jnp.bfloat16, jnp.float32, pltpu.SemaphoreType.DMA
    anywhere = pl.BlockSpec(memory_space=pl.ANY)
    shapes = (
        jax.ShapeDtypeStruct((block, width), f32),
        jax.ShapeDtypeStruct((block, width), f32),
        jax.ShapeDtypeStruct((rows, width), bf16),
    )
    results = pl.pallas_call(
        functools.partial(kernel, n, n_col),
        out_shape=shapes,
        in_specs=[anywhere] * 2,
        out_specs=(anywhere,) * 3,
        scratch_shapes=[
            pltpu.VMEM((rows, width), bf16),
            pltpu.VMEM((2, width, width), bf16),
            pltpu.VMEM((rows, half), bf16),
            pltpu.VMEM((rows, width), bf16),
            pltpu.VMEM((rows, width), f32),
            pltpu.VMEM((2, 2, units, block, reach), bf16),
            pltpu.VMEM((2, units, block, reach), bf16),
            pltpu.VMEM((2, units, block, reach), bf16),
            pltpu.VMEM((2, owned, groups - 1, block, reach), bf16),
            pltpu.VMEM((2, 4, 2, LANE, LANE), bf16),
            pltpu.VMEM((2, 4, 2, LANE, LANE), bf16),
            pltpu.VMEM((2, block, width), f32),
            pltpu.VMEM((1, width), f32),
            pltpu.VMEM((n - 1, 1, width), f32),
            pltpu.VMEM((rows, width), bf16),
            pltpu.VMEM((tiles, TILE, rows), bf16),
            dma((4,)),
            dma((half // TILE,)),
            dma((half // TILE,)),
            dma((2, sends)),
            dma((2, sends)),
            dma((2, sends)),
            dma((2, owned, groups - 1)),
            dma((2, 4, 2)),
            dma((2, 4, 2)),
            dma((n - 1,)),
            dma((n - 1,)),
            dma((2,)),
            dma((rows // TILE,)),
        ],
        compiler_params=pltpu.CompilerParams(
            collective_id=0, has_side_effects=True, vmem_limit_bytes=56 * 1024 * 1024
        ),
    )(snapshots, rotations)
    return pl.pallas_call(
        finish,
        out_shape=shapes,
        in_specs=[anywhere] * 3,
        out_specs=(anywhere,) * 3,
        scratch_shapes=[dma((12,))],
    )(*results)


def solution(mesh):
    return jax.shard_map(
        functools.partial(per_device, mesh.shape["row"], mesh.shape["col"]),
        mesh=mesh,
        in_specs=(P("row", "col"), P(None, "col", None)),
        out_specs=(P(("col", "row"), None), P(("col", "row"), None), P("row", "col")),
        check_vma=False,
    )
```

time: 63.8 us -> 157 us (2.46)
  the two profiles are of different devices: /device:TPU:0 before, /device:TPU:9 now
where the time goes in v2:
time: 157 us
  Pallas kernels  156 us (99%)
    pallas_call x1, Pallas kernels, per_device(): pl.pallas_call(finish, out_shape=shapes, in_specs=[anywhere] * 3, out_spe...  96.5 us
    pallas_call x1, Pallas kernels, per_device(): pl.pallas_call(functools.partial(kernel, n, n_col), out_shape=shapes, in_...  59.8 us

profile of v2, /device:TPU:9, one launch (start us, length us, event | category | flops | bytes accessed | tf_op | source)
XLA Modules:
  0.0 156.9 jit_solution(4416484847592962954)
XLA Ops:
  0.6 59.8 %shard_map.49 = (f32[128,1024]{1,0:T(8,128)}, f32[128,1024]{1,0:T(8,128)}, bf16[1024,1024]{1,0:T(8,128)(2,1)}) custom-call(bf16[1024,1024]{1,0:T(8,128)(2,1)} %x_hbm.1, bf16[2,1024,1024]{2,1,0:T(8,128)(2,1)} %rot_hbm.1), custom_call_target="tpu_custom_call" | custom-call | tf_op jit(solution)/shard_map/pallas_call | solution.py:409
  60.4 96.5 %shard_map.50 = (f32[128,1024]{1,0:T(8,128)}, f32[128,1024]{1,0:T(8,128)}, bf16[1024,1024]{1,0:T(8,128)(2,1)}) custom-call(f32[128,1024]{1,0:T(8,128)} %get-tuple-element.6.refs_0_, f32[128,1024]{1,0:T(8,128)} %get-tuple-element.7.refs_1_, bf16[1024,1024]{1,0:T(8,128)(2,1)} %get-tuple-element.8.refs_2_), custom_call_target="tpu_custom_call" | custom-call | tf_op jit(solution)/shard_map/pallas_call | solution.py:449

commit v3 on v2

--- a/solution.py
+++ b/solution.py
@@ -94,11 +94,9 @@
     ]
     load_x.wait()
     load_r0[0].wait()
-    for h in range(pieces):
-        turn(left, 0, h * TILE)
-        if h == 0:
-            pl.semaphore_wait(barrier, n + 1)
-        left_copy[h].start()
+    turn(left, 0, 0)
+    pl.semaphore_wait(barrier, n + 1)
+    left_copy[0].start()
 
     def owned(u):
         g = UNITS[u][0]
@@ -255,21 +253,29 @@
         return pltpu.make_async_copy(gram_out.at[s], target, store_sem.at[s])
 
     if symmetric:
-        for g in range(tiles):
+        due = []
+        for g in (0, 3, 2, 1):
+            now = [u for u in FIRST if UNITS[u][0] == g]
             flip(x, g)
-            pair_terms(0, x, [u for u in FIRST if UNITS[u][0] == g])
+            pair_terms(0, x, now)
+            pair_pass(0, due)
+            due = now
     else:
         rows_terms(0, x)
+    for h in range(1, pieces):
+        turn(left, 0, h * TILE)
+        left_copy[h].start()
+    if symmetric:
+        pair_pass(0, due)
+    else:
+        rows_pass(0)
     load_r0[1].wait()
     for h in range(pieces):
         turn(pair, 0, half + h * TILE)
     if symmetric:
-        pair_pass(0, FIRST)
         flip(pair, 2)
         flip(pair, 3)
         pair_terms(1, pair, STAGES[0])
-    else:
-        rows_pass(0)
 
     load_r1.wait()
 
@@ -372,20 +378,23 @@
 
 
 def finish(*refs):
-    sources, targets, sem = refs[:3], refs[3:6], refs[6]
-    copies = []
-    for source, target in zip(sources, targets):
-        pieces = 4 if source.shape[0] > 512 else 1
+    sources, targets, held, load_sem, store_sem = refs[:3], refs[3:6], refs[6:9], refs[9], refs[10]
+    loads, stores = [], []
+    for source, target, room in zip(sources, targets, held):
+        pieces = max(source.shape[0] // TILE, 1)
         size = source.shape[0] // pieces
         for p in range(pieces):
             span = pl.ds(p * size, size)
-            copies.append(
-                pltpu.make_async_copy(source.at[span], target.at[span], sem.at[len(copies)])
-            )
-    for copy in copies:
-        copy.start()
-    for copy in copies:
-        copy.wait()
+            at = len(loads)
+            loads.append(pltpu.make_async_copy(source.at[span], room.at[span], load_sem.at[at]))
+            stores.append(pltpu.make_async_copy(room.at[span], target.at[span], store_sem.at[at]))
+    for load in loads:
+        load.start()
+    for load, store in zip(loads, stores):
+        load.wait()
+        store.start()
+    for store in stores:
+        store.wait()
 
 
 def per_device(n, n_col, snapshots, rotations):
@@ -451,7 +460,8 @@
         out_shape=shapes,
         in_specs=[anywhere] * 3,
         out_specs=(anywhere,) * 3,
-        scratch_shapes=[dma((12,))],
+        scratch_shapes=[pltpu.VMEM(shape.shape, shape.dtype) for shape in shapes]
+        + [dma((2 + rows // TILE,))] * 2,
     )(*results)
 
 

time: 157 us -> 57.9 us (0.37)
  Pallas kernels: 156 us -> 57.1 us
    pallas_call x1, Pallas kernels: 96.5 us -> 2.8 us  [per_device(): pl.pallas_call(finish, out_shape=shapes, in_specs=[anywhere] * 3, out_spe...]
    pallas_call x1, Pallas kernels: 59.8 us -> 54.3 us  [per_device(): pl.pallas_call(functools.partial(kernel, n, n_col), out_shape=shapes, in_...]
where the time goes in v3:
time: 57.9 us; the launch traced here: 57.7 us
  Pallas kernels  57.1 us (99%)
  between operations  0.64 us (1%)
    pallas_call x1, Pallas kernels, per_device(): pl.pallas_call(functools.partial(kernel, n, n_col), out_shape=shapes, in_...  54.3 us
    pallas_call x1, Pallas kernels, per_device(): pl.pallas_call(finish, out_shape=shapes, in_specs=[anywhere] * 3, out_spe...  2.8 us

profile of v3, /device:TPU:9, one launch (start us, length us, event | category | flops | bytes accessed | tf_op | source)
XLA Modules:
  0.0 57.7 jit_solution(12132777965983475369)
XLA Ops:
  0.6 54.3 %shard_map.49 = (f32[128,1024]{1,0:T(8,128)}, f32[128,1024]{1,0:T(8,128)}, bf16[1024,1024]{1,0:T(8,128)(2,1)}) custom-call(bf16[1024,1024]{1,0:T(8,128)(2,1)} %x_hbm.1, bf16[2,1024,1024]{2,1,0:T(8,128)(2,1)} %rot_hbm.1), custom_call_target="tpu_custom_call" | custom-call | tf_op jit(solution)/shard_map/pallas_call | solution.py:418
  54.9 2.8 %shard_map.50 = (f32[128,1024]{1,0:T(8,128)}, f32[128,1024]{1,0:T(8,128)}, bf16[1024,1024]{1,0:T(8,128)(2,1)}) custom-call(f32[128,1024]{1,0:T(8,128)} %get-tuple-element.6.refs_0_, f32[128,1024]{1,0:T(8,128)} %get-tuple-element.7.refs_1_, bf16[1024,1024]{1,0:T(8,128)(2,1)} %get-tuple-element.8.refs_2_), custom_call_target="tpu_custom_call" | custom-call | tf_op jit(solution)/shard_map/pallas_call | solution.py:458

commit v4 on v3

--- a/solution.py
+++ b/solution.py
@@ -12,7 +12,7 @@
 
 UNITS = ((0, 0), (0, 2), (0, 3), (0, 1), (2, 2), (2, 3), (2, 1), (3, 3), (3, 1), (1, 1))
 FIRST = (0, 1, 2, 3, 4, 5, 6, 7, 8, 9)
-STAGES = ((4, 5, 7), (0, 1, 2), (3, 6, 8, 9))
+STAGES = ((4, 5, 7), (0, 1, 2), (8, 3, 6, 9))
 
 
 def kernel(
@@ -299,12 +299,12 @@
     if symmetric:
         flip(pair, 0)
         pair_terms(1, pair, STAGES[1])
+        pair_pass(1, STAGES[1])
     for h in range(pieces - 1):
         if h > 0:
             left_copy[h].wait_recv()
         add_moved(h * TILE, TILE, False)
     if symmetric:
-        pair_pass(1, STAGES[1])
         pair_sum(0, FIRST)
         pair_turned(0, FIRST)
     else:
@@ -316,6 +316,7 @@
     if symmetric:
         flip(pair, 1)
         pair_terms(1, pair, STAGES[2])
+        pair_pass(1, STAGES[2])
     else:
         rows_terms(1, pair)
     energy[...] = add_moved(half - TILE, TILE, False)
@@ -329,7 +330,6 @@
     for step in range(1, n):
         e_copy(step).start()
     if symmetric:
-        pair_pass(1, STAGES[2])
         pair_sum(1, STAGES[1])
         pair_turned(1, STAGES[0] + STAGES[1])
     else:

time: 57.9 us -> 57.8 us (level)
  no operation moved by 1% of the time
where the time goes in v4:
time: 57.8 us; the launch traced here: 57.6 us
  Pallas kernels  57 us (99%)
  between operations  0.64 us (1%)
    pallas_call x1, Pallas kernels, per_device(): pl.pallas_call(functools.partial(kernel, n, n_col), out_shape=shapes, in_...  54.2 us
    pallas_call x1, Pallas kernels, per_device(): pl.pallas_call(finish, out_shape=shapes, in_specs=[anywhere] * 3, out_spe...  2.8 us

profile of v4, /device:TPU:9, one launch (start us, length us, event | category | flops | bytes accessed | tf_op | source)
XLA Modules:
  0.0 57.6 jit_solution(3040557530401716808)
XLA Ops:
  0.6 54.2 %shard_map.49 = (f32[128,1024]{1,0:T(8,128)}, f32[128,1024]{1,0:T(8,128)}, bf16[1024,1024]{1,0:T(8,128)(2,1)}) custom-call(bf16[1024,1024]{1,0:T(8,128)(2,1)} %x_hbm.1, bf16[2,1024,1024]{2,1,0:T(8,128)(2,1)} %rot_hbm.1), custom_call_target="tpu_custom_call" | custom-call | tf_op jit(solution)/shard_map/pallas_call | solution.py:418
  54.8 2.8 %shard_map.50 = (f32[128,1024]{1,0:T(8,128)}, f32[128,1024]{1,0:T(8,128)}, bf16[1024,1024]{1,0:T(8,128)(2,1)}) custom-call(f32[128,1024]{1,0:T(8,128)} %get-tuple-element.6.refs_0_, f32[128,1024]{1,0:T(8,128)} %get-tuple-element.7.refs_1_, bf16[1024,1024]{1,0:T(8,128)(2,1)} %get-tuple-element.8.refs_2_), custom_call_target="tpu_custom_call" | custom-call | tf_op jit(solution)/shard_map/pallas_call | solution.py:458
